TPU v7x, 128 devices: a whole 4x4x4 slice. The times are simulated.
128 devices in a mesh: grp: 4 (over x), row: 32 (over z, y, core).
Axes of the slice: x: 4, y: 4, z: 4, core: 2. Of those that a mesh axis runs over, the one named last changes fastest.
Arguments:
- snapshots: bfloat16 [8192, 131072], P(None, ('grp', 'row')), may hold values from -8 to 8
- weights: float32 [131072], P(('grp', 'row')), may hold values from 0.25 to 4
- reference_field: float32 [131072], P(('grp', 'row')), may hold values from -6 to 6
- start_basis: float32 [64, 2, 63, 8], replicated, may hold values from -6 to 6
Outputs:
- spod_modes: float32 [64, 16, 131072], P(None, None, ('grp', 'row'))
- energies: float32 [64, 8], replicated
All inputs are finite; a program needn't handle non-finite values.
Results may differ from a plain program's by a relative error of at most 0.012.
The roundings to bfloat16 on the way count: a program that leaves them out, or rounds other values in their place, can miss the bound.
Values may be sent and summed in bfloat16 or wider, within the bound.
A program may use at most 192 MiB of HBM per device.

v0:
```python
import math
import jax
import jax.numpy as jnp
from jax import lax
from jax.sharding import PartitionSpec as P

NFFT = 256
NBLK = 63
NF = 64
NM = 8
ITERS = 12
highest = lax.Precision.HIGHEST


def dft_table():
    time_steps = jnp.arange(NFFT, dtype=jnp.int32)
    freq_bins = jnp.arange(1, NF + 1, dtype=jnp.int32)
    wrapped = freq_bins[:, None] * time_steps[None, :] % NFFT
    angles = 2.0 * math.pi / NFFT * wrapped.astype(jnp.float32)
    window_taper = 0.5 - 0.5 * jnp.cos(2.0 * math.pi / NFFT * time_steps.astype(jnp.float32))
    scaled_taper = window_taper / jnp.sqrt(jnp.sum(window_taper * window_taper))
    stacked = jnp.stack([jnp.cos(angles), -jnp.sin(angles)]) * scaled_taper[None, None, :]
    return stacked.astype(jnp.bfloat16)


def apply_gram(gram_real, gram_imag, basis_real, basis_imag):
    image_real = jnp.einsum("fbc,fck->fbk", gram_real, basis_real, precision=highest) - jnp.einsum(
        "fbc,fck->fbk", gram_imag, basis_imag, precision=highest
    )
    image_imag = jnp.einsum("fbc,fck->fbk", gram_real, basis_imag, precision=highest) + jnp.einsum(
        "fbc,fck->fbk", gram_imag, basis_real, precision=highest
    )
    return (image_real, image_imag)


def orthonormalize(image_real, image_imag):
    cols_real = []
    cols_imag = []
    for column in range(image_real.shape[2]):
        target_real = image_real[:, :, column]
        target_imag = image_imag[:, :, column]
        for earlier in range(column):
            prior_real = cols_real[earlier]
            prior_imag = cols_imag[earlier]
            inner_real = jnp.sum(
                prior_real * target_real + prior_imag * target_imag, axis=1, keepdims=True
            )
            inner_imag = jnp.sum(
                prior_real * target_imag - prior_imag * target_real, axis=1, keepdims=True
            )
            target_real, target_imag = (
                target_real - (inner_real * prior_real - inner_imag * prior_imag),
                target_imag - (inner_real * prior_imag + inner_imag * prior_real),
            )
        length = jnp.sqrt(
            jnp.sum(target_real * target_real + target_imag * target_imag, axis=1, keepdims=True)
            + 1e-06
        )
        cols_real.append(target_real / length)
        cols_imag.append(target_imag / length)
    return (jnp.stack(cols_real, axis=2), jnp.stack(cols_imag, axis=2))


def subspace_solve(gram_real, gram_imag, start_basis):

    def sweep_once(sweep_index, current):
        image_real, image_imag = apply_gram(gram_real, gram_imag, current[0], current[1])
        return orthonormalize(image_real, image_imag)

    basis_real, basis_imag = lax.fori_loop(
        0, ITERS, sweep_once, (start_basis[:, 0], start_basis[:, 1])
    )
    image_real, image_imag = apply_gram(gram_real, gram_imag, basis_real, basis_imag)
    energy = jnp.sum(basis_real * image_real + basis_imag * image_imag, axis=1)
    return (basis_real, basis_imag, energy)


def coefficient_matrix(basis_real, basis_imag):
    round_real = basis_real.astype(jnp.bfloat16)
    round_imag = basis_imag.astype(jnp.bfloat16)
    upper_half = jnp.concatenate([round_real, round_imag], axis=2)
    lower_half = jnp.concatenate([-round_imag, round_real], axis=2)
    return jnp.stack([upper_half, lower_half], axis=1)


def phase_turn(correlation, energy):
    gain_scale = 1.0 / jnp.sqrt(energy + 1e-06)
    tilt_real = gain_scale * correlation[:, :NM]
    tilt_imag = gain_scale * correlation[:, NM:]
    tilt_size = jnp.sqrt(jnp.maximum(tilt_real * tilt_real + tilt_imag * tilt_imag, 0.25))
    return (gain_scale * tilt_real / tilt_size, -gain_scale * tilt_imag / tilt_size)


def finish(projected, factor_real, factor_imag, root_weight):
    part_real = projected[:, :NM]
    part_imag = projected[:, NM:]
    inverse_root = 1.0 / root_weight
    out_real = (
        part_real * factor_real[:, :, None] - part_imag * factor_imag[:, :, None]
    ) * inverse_root
    out_imag = (
        part_real * factor_imag[:, :, None] + part_imag * factor_real[:, :, None]
    ) * inverse_root
    return jnp.concatenate([out_real, out_imag], axis=1)


def shards(snapshots, weights, reference_field, start_basis):
    dft_rows = dft_table()
    half_len = NFFT // 2
    rows_here = snapshots.shape[1]
    total_rows = rows_here * lax.axis_size(("grp", "row"))
    hop_rows = snapshots.reshape(NBLK + 1, half_len, rows_here)
    root_weight = jnp.sqrt(weights)
    leading = jnp.einsum(
        "pft,htx->fphx",
        dft_rows[:, :, :half_len],
        hop_rows[:NBLK],
        preferred_element_type=jnp.float32,
    )
    trailing = jnp.einsum(
        "pft,htx->fphx", dft_rows[:, :, half_len:], hop_rows[1:], preferred_element_type=jnp.float32
    )
    coeffs = ((leading + trailing) * root_weight).astype(jnp.bfloat16)
    real_part = jnp.einsum("fpbx,fpcx->fbc", coeffs, coeffs, preferred_element_type=jnp.float32)
    cross_part = jnp.einsum(
        "fbx,fcx->fbc", coeffs[:, 0], coeffs[:, 1], preferred_element_type=jnp.float32
    )
    cross_anti = cross_part - jnp.swapaxes(cross_part, 1, 2)
    gram_part = jnp.concatenate([real_part, cross_anti], axis=2)
    probe = (root_weight * reference_field).astype(jnp.bfloat16)
    projection_part = jnp.einsum("fpbx,x->fpb", coeffs, probe, preferred_element_type=jnp.float32)
    summed = lax.psum(gram_part, ("grp", "row"))
    gram_real = summed[:, :NBLK, :NBLK] / total_rows
    gram_imag = summed[:, :NBLK, NBLK:] / total_rows
    basis_real, basis_imag, energy = subspace_solve(gram_real, gram_imag, start_basis)
    local_matrix = coefficient_matrix(basis_real, basis_imag)
    extras = energy[:, None, :]
    energies = extras[:, 0]
    projected = jnp.einsum(
        "fpbk,fpbx->fkx", local_matrix, coeffs, preferred_element_type=jnp.float32
    )
    projection = lax.psum(projection_part, ("grp", "row")) / math.sqrt(total_rows)
    correlation = jnp.einsum(
        "fpb,fpbk->fk", projection, local_matrix.astype(jnp.float32), precision=highest
    )
    factor_real, factor_imag = phase_turn(correlation, energies)
    return (finish(projected, factor_real, factor_imag, root_weight), energies)


def solution(mesh):
    in_specs = (P(None, ("grp", "row")), P(("grp", "row")), P(("grp", "row")), P())
    out_specs = (P(None, None, ("grp", "row")), P())
    return jax.shard_map(shards, mesh=mesh, in_specs=in_specs, out_specs=out_specs, check_vma=False)
```

profile of v0, /device:TPU:1, one launch (start us, length us, event | category | flops | bytes accessed | tf_op | source)
XLA Modules:
  0.0 661.7 jit_solution(498211603777411236)
XLA Ops:
  9.0 23.1 %fusion.84 = (bf16[8064,1024]{1,0:T(8,128)(2,1)}, bf16[8064,1024]{1,0:T(8,128)(2,1)}) fusion(bf16[8192,1024]{1,0:T(8,128)(2,1)} %param.6), kind=kLoop, calls=%fused_computation.327 | loop fusion | bytes 66060288 | tf_op jit(solution)/shard_map/slice | solution.py:121
  32.1 21.0 %fusion.72 = f32[2,64,63,1024]{3,1,2,0:T(8,128)} fusion(bf16[63,128,1024,1]{2,1,0,3:T(8,128)(2,1)} %bitcast.408, bf16[2,64,256]{2,1,0:T(8,128)(2,1)S(1)} %fusion.65), kind=kOutput, calls=%fused_computation.304 | convolution fusion | flops 2113929216 | bytes 49577984 | tf_op jit(solution)/shard_map/pft,htx->fphx/dot_general | solution.py:114
  53.2 23.1 %fusion.50 = bf16[64,2,63,1024]{3,0,2,1:T(8,128)(2,1)} fusion(f32[1024]{0:T(1024)S(1)} %get-tuple-element.268, f32[2,64,63,1024]{3,1,2,0:T(8,128)} %fusion.72, bf16[63,128,1024,1]{2,1,0,3:T(8,128)(2,1)} %bitcast.407, bf16[2,64,256]{2,1,0:T(8,128)(2,1)S(1)} %fusion.65), kind=kOutput, calls=%fused_computation.263 | convolution fusion | flops 2138701824 | bytes 66097152 | tf_op jit(solution)/shard_map/pft,htx->fphx/dot_general | solution.py:120
  76.3 12.3 %slice_bitcast_fusion.1 = (bf16[64,63,1024]{2,0,1:T(8,128)(2,1)}, bf16[64,63,1024]{2,0,1:T(8,128)(2,1)}) fusion(bf16[64,2,63,1024]{3,0,2,1:T(8,128)(2,1)} %fusion.50), kind=kLoop, calls=%fused_computation.268 | loop fusion | bytes 33030144 | tf_op jit(solution)/shard_map/squeeze | solution.py:126
  88.5 33.2 %fusion.57 = f32[64,63,63]{2,1,0:T(8,128)} fusion(bf16[64,2,63,1024]{3,0,2,1:T(8,128)(2,1)} %fusion.50), kind=kOutput, calls=%fused_computation.277 | convolution fusion | flops 1040449536 | bytes 17531136 | tf_op jit(solution)/shard_map/fpbx,fpcx->fbc/dot_general | solution.py:124
  121.8 14.4 %fusion.51 = f32[64,63,63]{2,1,0:T(8,128)S(1)} fusion(bf16[64,63,1024]{2,0,1:T(8,128)(2,1)} %get-tuple-element.255, bf16[64,63,1024]{2,0,1:T(8,128)(2,1)} %get-tuple-element.254), kind=kOutput, calls=%fused_computation.264 | convolution fusion | flops 520224768 | bytes 17531136 | tf_op jit(solution)/shard_map/fbx,fcx->fbc/dot_general | solution.py:125
  142.4 10.0 %fusion.74 = f32[1,64,2,63]{1,0,3,2:T(1,128)S(1)} fusion(bf16[64,2,63,1024]{3,0,2,1:T(8,128)(2,1)} %fusion.50, bf16[1024,1,1,1]{0,1,2,3:T(2,128)(2,1)S(1)} %reshape.3858), kind=kOutput, calls=%fused_computation.309 | convolution fusion | flops 16515072 | bytes 16549376 | tf_op jit(solution)/shard_map/fpbx,x->fpb/dot_general | solution.py:131
  152.5 69.7 %psum.15 = f32[64,2,63]{2,1,0:T(2,128)S(1)} all-reduce(f32[64,2,63]{2,1,0:T(2,128)S(1)} %bitcast.409), channel_id=1, replica_groups=mesh['grp'=4,'row'=32] {'grp','row'}, use_global_device_ids=true, to_apply=%region_69.70 | all-reduce | flops 8064 | bytes 64512 | tf_op jit(solution)/shard_map/psum | solution.py:142
  223.7 73.2 %all-reduce.2.cloned.1.call-done = f32[64,63,126]{2,1,0:T(8,128)} async-done(((f32[64,63,126]{2,1,0:T(8,128)}), f32[64,63,126]{2,1,0:T(8,128)}) %all-reduce.2.cloned.1.call-update) | async-done | bytes 2032144 | tf_op jit(solution)/shard_map/psum | solution.py:132
  296.8 4.4 slice_multiply_fusion
  301.2 299.5 %while.12 = (s32[]{:T(128)}, f32[64,63,8]{0,2,1:T(8,128)}, f32[64,63,8]{0,2,1:T(8,128)}, f32[64,63,63]{2,1,0:T(8,128)}, f32[64,63,63]{2,1,0:T(8,128)S(1)}, /*index=5*/s32[]{:T(128)}) while((s32[]{:T(128)}, f32[64,63,8]{0,2,1:T(8,128)}, f32[64,63,8]{0,2,1:T(8,128)}, f32[64,63,63]{2,1,0:T(8,128)}, f32[64,63,63]{2,1,0:T(8,128)S(1)}, ...), condition=%wide.region_67.68_spmd, body=%wide.region_2.67_spmd.sunk | while | flops 100723840 | bytes 13749573 | solution.py:70
  302.7 4.9 fusion.131
  312.8 4.9 fusion.134
  317.9 3.4 fusion.135
  327.7 4.9 fusion.131
  337.7 4.9 fusion.134
  342.8 3.4 fusion.135
  352.6 4.9 fusion.131
  362.6 4.9 fusion.134
  367.7 3.4 fusion.135
  377.5 4.9 fusion.131
  387.5 4.9 fusion.134
  392.6 3.4 fusion.135
  402.4 4.9 fusion.131
  412.4 4.9 fusion.134
  417.6 3.4 fusion.135
  427.3 4.9 fusion.131
  437.3 4.9 fusion.134
  442.5 3.4 fusion.135
  452.2 4.9 fusion.131
  462.3 4.9 fusion.134
  467.4 3.4 fusion.135
  477.1 4.9 fusion.131
  487.2 4.9 fusion.134
  492.3 3.4 fusion.135
  502.0 4.9 fusion.131
  512.1 4.9 fusion.134
  527.0 4.9 fusion.131
  537.0 4.9 fusion.134
  542.1 3.4 fusion.135
  551.9 4.9 fusion.131
  561.9 4.9 fusion.134
  576.8 4.9 fusion.131
  586.8 4.9 fusion.134
  603.2 4.9 fusion.80
  611.5 3.5 fusion.60
  615.0 3.6 fusion.63
  618.8 29.5 %fusion.54 = f32[64,16,1024]{2,1,0:T(8,128)} fusion(bf16[64,2,63,1024]{3,0,2,1:T(8,128)(2,1)} %fusion.50, bf16[64,1,63,16]{2,3,1,0:T(8,128)(2,1)S(1)} %get-tuple-element.263, bf16[64,1,63,16]{2,3,1,0:T(8,128)(2,1)S(1)} %get-tuple-element.262), kind=kOutput, calls=%fused_computation.270 | convolution fusion | flops 264370176 | bytes 20967424 | tf_op jit(solution)/shard_map/fpbk,fpbx->fkx/dot_general | solution.py:139
  (766 shorter events, 168.7 us)
Async XLA Ops:
  7.2 289.7 %all-reduce.2.cloned.1.call-start = ((), (), s32[]{:S(2)}) async-start(), calls=%async_computation | async-start | bytes 4194304 | tf_op jit(solution)/shard_map/psum | solution.py:132
  32.1 21.1 %copy-start.5 = (f32[1024]{0:T(1024)S(1)}, f32[1024]{0:T(1024)}, u32[]{:S(2)}) copy-start(f32[1024]{0:T(1024)} %param.8) | copy-start | bytes 12292
  32.1 21.1 %copy-start.6 = (f32[1024]{0:T(1024)S(1)}, f32[1024]{0:T(1024)}, u32[]{:S(2)}) copy-start(f32[1024]{0:T(1024)} %param.7) | copy-start | bytes 12292
  138.2 2.2 copy-start.1
  142.4 80.5 %copy-start.2 = (f32[64,2,63,8]{0,3,2,1:T(8,128)S(1)}, f32[64,2,63,8]{0,3,2,1:T(8,128)}, u32[]{:S(2)}) copy-start(f32[64,2,63,8]{0,3,2,1:T(8,128)} %param.9) | copy-start | bytes 774148
  601.9 6.3 copy-start
  618.7 30.2 %copy-start.4 = (f32[64,8]{0,1:T(8,128)}, f32[64,8]{0,1:T(8,128)S(1)}, u32[]{:S(2)}) copy-start(f32[64,8]{0,1:T(8,128)S(1)} %copy.354) | copy-start | bytes 6148
  618.8 29.5 %copy-start.3 = (f32[64,2,63]{2,1,0:T(2,128)S(1)}, f32[64,2,63]{2,1,0:T(2,128)}, u32[]{:S(2)}) copy-start(f32[64,2,63]{2,1,0:T(2,128)} %broadcast_multiply_fusion.13) | copy-start | bytes 96772
Sparse Core Ops, SparseCore 0:
  142.5 154.2 all-reduce.1
where the time goes:
time: 669 us; the launch traced here: 662 us
  matrix products  346 us (52%)
  local copies, waits for them, and re-layouts  107 us (16%)
  waiting for transfers between devices  73.2 us (11%)
  blocking collectives  69.7 us (10%)
  other arithmetic  47 us (7%)
  between operations  15.1 us (2%)
    psum x1, waiting for transfers between devices, shards(): summed = lax.psum(gram_part, ('grp', 'row'))  73.2 us
    psum x1, blocking collectives, shards(): lax.psum(projection_part, ('grp', 'row')) / math.sqrt(total_rows)  69.7 us
    dot_general x13, matrix products, apply_gram(): jnp.einsum('fbc,fck->fbk', gram_real, basis_real, precision=highest)  64.2 us
    dot_general x13, matrix products, apply_gram(): jnp.einsum('fbc,fck->fbk', gram_real, basis_imag, precision=highest)  62.7 us
    dot_general x13, matrix products, apply_gram(): jnp.einsum('fbc,fck->fbk', gram_imag, basis_real, precision=highest)  43.9 us
    dot_general x13, matrix products, apply_gram(): jnp.einsum('fbc,fck->fbk', gram_imag, basis_imag, precision=highest)  43.8 us
    dot_general x1, matrix products, shards(): jnp.einsum('fpbx,fpcx->fbc', coeffs, coeffs, preferred_element_type=jnp.f...  33.2 us
    dot_general x1, matrix products, shards(): jnp.einsum('fpbk,fpbx->fkx', local_matrix, coeffs, preferred_element_type...  29.5 us
  transfers between devices with their start and end apart: 1, of which 1 were waited for; matrix products, arithmetic and copies ran while one was open for 2% of the time, Pallas kernels for 0%

commit v1 on v0

--- a/solution.py
+++ b/solution.py
@@ -10,6 +10,11 @@
 NM = 8
 ITERS = 12
 highest = lax.Precision.HIGHEST
+
+
+def one_after_other(value, inner_axis, outer_axis):
+    half = lax.psum(value, inner_axis)
+    return lax.psum(half, outer_axis)
 
 
 def dft_table():
@@ -139,7 +144,7 @@
     projected = jnp.einsum(
         "fpbk,fpbx->fkx", local_matrix, coeffs, preferred_element_type=jnp.float32
     )
-    projection = lax.psum(projection_part, ("grp", "row")) / math.sqrt(total_rows)
+    projection = one_after_other(projection_part, "grp", "row") / math.sqrt(total_rows)
     correlation = jnp.einsum(
         "fpb,fpbk->fk", projection, local_matrix.astype(jnp.float32), precision=highest
     )

time: 669 us -> 670 us (level)
  blocking collectives: 69.7 us -> 140 us
  waiting for transfers between devices: 73.2 us -> 3.03 us
    psum x1 -> x2, blocking collectives: 69.7 us -> 140 us  [the longest x1 125 us: one_after_other(): return lax.psum(half, outer_axis)]
    psum x1, waiting for transfers between devices: 73.2 us -> 3.01 us  [shards(): summed = lax.psum(gram_part, ('grp', 'row'))]
where the time goes in v1:
time: 670 us; the launch traced here: 662 us
  matrix products  346 us (52%)
  blocking collectives  140 us (21%)
  local copies, waits for them, and re-layouts  107 us (16%)
  other arithmetic  47 us (7%)
  between operations  15.1 us (2%)
    psum x1, blocking collectives, one_after_other(): return lax.psum(half, outer_axis)  125 us
    dot_general x13, matrix products, apply_gram(): jnp.einsum('fbc,fck->fbk', gram_real, basis_real, precision=highest)  64.2 us
    dot_general x13, matrix products, apply_gram(): jnp.einsum('fbc,fck->fbk', gram_real, basis_imag, precision=highest)  62.7 us
    dot_general x13, matrix products, apply_gram(): jnp.einsum('fbc,fck->fbk', gram_imag, basis_real, precision=highest)  43.9 us
    dot_general x13, matrix products, apply_gram(): jnp.einsum('fbc,fck->fbk', gram_imag, basis_imag, precision=highest)  43.8 us
    dot_general x1, matrix products, shards(): jnp.einsum('fpbx,fpcx->fbc', coeffs, coeffs, preferred_element_type=jnp.f...  33.2 us
    dot_general x1, matrix products, shards(): jnp.einsum('fpbk,fpbx->fkx', local_matrix, coeffs, preferred_element_type...  29.5 us
    another operation x24, local copies, waits for them, and re-layouts  26.7 us
  transfers between devices with their start and end apart: 1, of which 1 were waited for; matrix products, arithmetic and copies ran while one was open for 2% of the time, Pallas kernels for 0%

profile of v1, /device:TPU:1, one launch (start us, length us, event | category | flops | bytes accessed | tf_op | source)
XLA Modules:
  0.0 661.7 jit_solution(5132275046788033403)
XLA Ops:
  9.0 23.1 %fusion.84 = (bf16[8064,1024]{1,0:T(8,128)(2,1)}, bf16[8064,1024]{1,0:T(8,128)(2,1)}) fusion(bf16[8192,1024]{1,0:T(8,128)(2,1)} %param.6), kind=kLoop, calls=%fused_computation.327 | loop fusion | bytes 66060288 | tf_op jit(solution)/shard_map/slice | solution.py:126
  32.1 21.0 %fusion.72 = f32[2,64,63,1024]{3,1,2,0:T(8,128)} fusion(bf16[63,128,1024,1]{2,1,0,3:T(8,128)(2,1)} %bitcast.408, bf16[2,64,256]{2,1,0:T(8,128)(2,1)S(1)} %fusion.65), kind=kOutput, calls=%fused_computation.304 | convolution fusion | flops 2113929216 | bytes 49577984 | tf_op jit(solution)/shard_map/pft,htx->fphx/dot_general | solution.py:119
  53.2 23.1 %fusion.50 = bf16[64,2,63,1024]{3,0,2,1:T(8,128)(2,1)} fusion(f32[1024]{0:T(1024)S(1)} %get-tuple-element.268, f32[2,64,63,1024]{3,1,2,0:T(8,128)} %fusion.72, bf16[63,128,1024,1]{2,1,0,3:T(8,128)(2,1)} %bitcast.407, bf16[2,64,256]{2,1,0:T(8,128)(2,1)S(1)} %fusion.65), kind=kOutput, calls=%fused_computation.263 | convolution fusion | flops 2138701824 | bytes 66097152 | tf_op jit(solution)/shard_map/pft,htx->fphx/dot_general | solution.py:125
  76.3 12.3 %slice_bitcast_fusion.1 = (bf16[64,63,1024]{2,0,1:T(8,128)(2,1)}, bf16[64,63,1024]{2,0,1:T(8,128)(2,1)}) fusion(bf16[64,2,63,1024]{3,0,2,1:T(8,128)(2,1)} %fusion.50), kind=kLoop, calls=%fused_computation.268 | loop fusion | bytes 33030144 | tf_op jit(solution)/shard_map/squeeze | solution.py:131
  88.5 33.2 %fusion.57 = f32[64,63,63]{2,1,0:T(8,128)} fusion(bf16[64,2,63,1024]{3,0,2,1:T(8,128)(2,1)} %fusion.50), kind=kOutput, calls=%fused_computation.277 | convolution fusion | flops 1040449536 | bytes 17531136 | tf_op jit(solution)/shard_map/fpbx,fpcx->fbc/dot_general | solution.py:129
  121.8 14.4 %fusion.51 = f32[64,63,63]{2,1,0:T(8,128)S(1)} fusion(bf16[64,63,1024]{2,0,1:T(8,128)(2,1)} %get-tuple-element.255, bf16[64,63,1024]{2,0,1:T(8,128)(2,1)} %get-tuple-element.254), kind=kOutput, calls=%fused_computation.264 | convolution fusion | flops 520224768 | bytes 17531136 | tf_op jit(solution)/shard_map/fbx,fcx->fbc/dot_general | solution.py:130
  142.4 10.0 %fusion.74 = f32[1,64,2,63]{1,0,3,2:T(1,128)S(1)} fusion(bf16[64,2,63,1024]{3,0,2,1:T(8,128)(2,1)} %fusion.50, bf16[1024,1,1,1]{0,1,2,3:T(2,128)(2,1)S(1)} %reshape.3858), kind=kOutput, calls=%fused_computation.309 | convolution fusion | flops 16515072 | bytes 16549376 | tf_op jit(solution)/shard_map/fpbx,x->fpb/dot_general | solution.py:136
  152.5 14.6 %psum.22 = f32[64,2,63]{2,1,0:T(2,128)S(1)} all-reduce(f32[64,2,63]{2,1,0:T(2,128)S(1)} %bitcast.409), channel_id=1, replica_groups=mesh['grp'=4,'row'=32] {'grp'}, use_global_device_ids=true, to_apply=%region_69.70 | all-reduce | flops 8064 | bytes 64512 | tf_op jit(solution)/shard_map/psum | solution.py:16
  167.2 125.2 %psum.23 = f32[64,2,63]{2,1,0:T(2,128)S(1)} all-reduce(f32[64,2,63]{2,1,0:T(2,128)S(1)} %psum.22), channel_id=1, replica_groups=mesh['grp'=4,'row'=32] {'row'}, use_global_device_ids=true, to_apply=%region_70.71 | all-reduce | flops 8064 | bytes 64512 | tf_op jit(solution)/shard_map/psum | solution.py:17
  296.9 4.4 slice_multiply_fusion
  301.3 299.5 %while.12 = (s32[]{:T(128)}, f32[64,63,8]{0,2,1:T(8,128)}, f32[64,63,8]{0,2,1:T(8,128)}, f32[64,63,63]{2,1,0:T(8,128)}, f32[64,63,63]{2,1,0:T(8,128)S(1)}, /*index=5*/s32[]{:T(128)}) while((s32[]{:T(128)}, f32[64,63,8]{0,2,1:T(8,128)}, f32[64,63,8]{0,2,1:T(8,128)}, f32[64,63,63]{2,1,0:T(8,128)}, f32[64,63,63]{2,1,0:T(8,128)S(1)}, ...), condition=%wide.region_67.68_spmd, body=%wide.region_2.67_spmd.sunk | while | flops 100723840 | bytes 13749573 | solution.py:75
  302.8 4.9 fusion.131
  312.8 4.9 fusion.134
  317.9 3.4 fusion.135
  327.7 4.9 fusion.131
  337.7 4.9 fusion.134
  342.8 3.4 fusion.135
  352.6 4.9 fusion.131
  362.6 4.9 fusion.134
  367.8 3.4 fusion.135
  377.5 4.9 fusion.131
  387.5 4.9 fusion.134
  392.7 3.4 fusion.135
  402.4 4.9 fusion.131
  412.5 4.9 fusion.134
  417.6 3.4 fusion.135
  427.3 4.9 fusion.131
  437.4 4.9 fusion.134
  442.5 3.4 fusion.135
  452.2 4.9 fusion.131
  462.3 4.9 fusion.134
  467.4 3.4 fusion.135
  477.2 4.9 fusion.131
  487.2 4.9 fusion.134
  502.1 4.9 fusion.131
  512.1 4.9 fusion.134
  517.2 3.4 fusion.135
  527.0 4.9 fusion.131
  537.0 4.9 fusion.134
  551.9 4.9 fusion.131
  561.9 4.9 fusion.134
  567.1 3.4 fusion.135
  576.8 4.9 fusion.131
  586.8 4.9 fusion.134
  603.2 4.9 fusion.80
  611.5 3.5 fusion.60
  615.0 3.6 fusion.63
  618.8 29.5 %fusion.54 = f32[64,16,1024]{2,1,0:T(8,128)} fusion(bf16[64,2,63,1024]{3,0,2,1:T(8,128)(2,1)} %fusion.50, bf16[64,1,63,16]{2,3,1,0:T(8,128)(2,1)S(1)} %get-tuple-element.263, bf16[64,1,63,16]{2,3,1,0:T(8,128)(2,1)S(1)} %get-tuple-element.262), kind=kOutput, calls=%fused_computation.270 | convolution fusion | flops 264370176 | bytes 20967424 | tf_op jit(solution)/shard_map/fpbk,fpbx->fkx/dot_general | solution.py:144
  (767 shorter events, 171.7 us)
Async XLA Ops:
  7.2 289.7 %all-reduce.2.cloned.1.call-start = ((), (), s32[]{:S(2)}) async-start(), calls=%async_computation | async-start | bytes 4194304 | tf_op jit(solution)/shard_map/psum | solution.py:137
  32.1 21.1 %copy-start.5 = (f32[1024]{0:T(1024)S(1)}, f32[1024]{0:T(1024)}, u32[]{:S(2)}) copy-start(f32[1024]{0:T(1024)} %param.8) | copy-start | bytes 12292
  32.1 21.1 %copy-start.6 = (f32[1024]{0:T(1024)S(1)}, f32[1024]{0:T(1024)}, u32[]{:S(2)}) copy-start(f32[1024]{0:T(1024)} %param.7) | copy-start | bytes 12292
  138.2 2.2 copy-start.1
  142.4 150.6 %copy-start.2 = (f32[64,2,63,8]{0,3,2,1:T(8,128)S(1)}, f32[64,2,63,8]{0,3,2,1:T(8,128)}, u32[]{:S(2)}) copy-start(f32[64,2,63,8]{0,3,2,1:T(8,128)} %param.9) | copy-start | bytes 774148
  601.9 6.3 copy-start
  618.7 30.2 %copy-start.4 = (f32[64,8]{0,1:T(8,128)}, f32[64,8]{0,1:T(8,128)S(1)}, u32[]{:S(2)}) copy-start(f32[64,8]{0,1:T(8,128)S(1)} %copy.354) | copy-start | bytes 6148
  618.8 29.5 %copy-start.3 = (f32[64,2,63]{2,1,0:T(2,128)S(1)}, f32[64,2,63]{2,1,0:T(2,128)}, u32[]{:S(2)}) copy-start(f32[64,2,63]{2,1,0:T(2,128)} %broadcast_multiply_fusion.13) | copy-start | bytes 96772
Sparse Core Ops, SparseCore 0:
  142.5 154.3 all-reduce.1
